TPU v7x, 32 devices: a whole 2x2x4 slice. The times are simulated.
32 devices in a mesh: dp: 4 (over y, core), owner: 8 (over z, x).
Axes of the slice: x: 2, y: 2, z: 4, core: 2. Of those that a mesh axis runs over, the one named last changes fastest.
Arguments:
- activations: bfloat16 [8192, 8192], P('dp', 'owner'), may hold values from -6 to 6
- ffn_grads: bfloat16 [8192, 16384], P('dp', 'owner'), may hold values from -6 to 6
- lengths: int32 [4, 16], P('dp'), may hold values from 1 to 512, 2048 in all within a row
- sample_pos: int32 [4, 16, 16], P('dp'), may hold values from 0 to 1048575
Outputs:
- chol_in: float32 [8192, 1536], P('owner')
- chol_out: float32 [16384, 1536], P('owner')
Inputs may be any that keep to these rules, and one draw needn't show every extreme that they name: Each dp index's document lengths sum to 2048; the longest is exactly 512.
All inputs are finite; a program needn't handle non-finite values.
Results may differ from a plain program's by a relative error of at most 0.0019.
Values may be sent and summed in bfloat16 or wider, within the bound.
No kernel may reach another device: no remote copies, remote signals or barrier semaphores. Data moves between devices by JAX's collectives and lax.ppermute only.
A program may use at most 192 MiB of HBM per device.

v0:
```python
import jax
import jax.numpy as jnp
from jax import lax
from jax.sharding import PartitionSpec as P

PB = 512
NPAN = 3
SAMP_DOC = 16


DAMPING = 0.1


def broadcast(shard, axis, root):
    mine = lax.axis_index(axis) == root
    return lax.psum(jnp.where(mine, shard, jnp.zeros_like(shard)), axis)


def window_columns(sampled):
    width = sampled.shape[1]
    gathered = []
    for column in range(NPAN):
        first_col = column * PB
        owner_root = first_col // width
        offset = first_col % width
        gathered.append(broadcast(sampled[:, offset : offset + PB], "owner", owner_root))
    return jnp.concatenate(gathered, axis=1)


def damped(gram):
    height = gram.shape[0]
    global_row = lax.axis_index("owner") * height + jnp.arange(height, dtype=jnp.int32)
    cols = jnp.arange(gram.shape[1], dtype=jnp.int32)
    return gram + DAMPING * (global_row[:, None] == cols[None, :]).astype(jnp.float32)


def factorize(gram):
    height = gram.shape[0]
    global_row = lax.axis_index("owner") * height + jnp.arange(height, dtype=jnp.int32)
    triangle = jnp.zeros_like(gram)
    for column in range(NPAN):
        first_col = column * PB
        end_col = first_col + PB
        owner_root = first_col // height
        offset = first_col % height
        local_row = triangle[offset : offset + PB, :first_col]
        pivot_in = gram[offset : offset + PB, first_col:end_col] - jnp.dot(
            local_row, local_row.T, precision=lax.Precision.HIGHEST
        )
        pivot = jnp.linalg.cholesky(pivot_in)
        outgoing = jnp.concatenate([local_row, pivot], axis=1)
        received = broadcast(outgoing, "owner", owner_root)
        previous = received[:, :first_col]
        pivot_got = received[:, first_col:end_col]
        residual = gram[:, first_col:end_col] - jnp.dot(
            triangle[:, :first_col], previous.T, precision=lax.Precision.HIGHEST
        )
        solved = lax.linalg.triangular_solve(
            pivot_got, residual, left_side=False, lower=True, transpose_a=True
        )
        inside = jnp.take(pivot_got, jnp.clip(global_row - first_col, 0, PB - 1), axis=0)
        solved = jnp.where(
            (global_row < first_col)[:, None],
            0.0,
            jnp.where((global_row < end_col)[:, None], inside, solved),
        )
        triangle = triangle.at[:, first_col:end_col].set(solved)
    return triangle


def local(activations, ffn_grads, lengths, sample_pos):
    total = activations.shape[0] * lax.axis_size("dp")
    doc_len = lengths[0]
    doc_start = jnp.cumsum(doc_len) - doc_len
    row_index = (doc_start[:, None] + jnp.remainder(sample_pos[0], doc_len[:, None])).reshape(-1)
    weight = jnp.broadcast_to(
        (doc_len.astype(jnp.float32) / (SAMP_DOC * total))[:, None], sample_pos[0].shape
    ).reshape(-1)
    sampled_in = jnp.take(activations, row_index, axis=0)
    sampled_out = jnp.take(ffn_grads, row_index, axis=0)
    scaled_in = (weight[:, None] * sampled_in.astype(jnp.float32)).astype(jnp.bfloat16)
    scaled_out = (weight[:, None] * sampled_out.astype(jnp.float32)).astype(jnp.bfloat16)
    window_in = window_columns(sampled_in)
    window_out = window_columns(sampled_out)
    part_in = jnp.einsum("rb,rk->bk", scaled_in, window_in, preferred_element_type=jnp.float32)
    part_out = jnp.einsum("rb,rk->bk", scaled_out, window_out, preferred_element_type=jnp.float32)
    share_in, share_out = (
        lax.psum_scatter(part_in, "dp", scatter_dimension=0, tiled=True),
        lax.psum_scatter(part_out, "dp", scatter_dimension=0, tiled=True),
    )
    gram_in, gram_out = (
        lax.all_gather(share_in, "dp", axis=0, tiled=True),
        lax.all_gather(share_out, "dp", axis=0, tiled=True),
    )
    return (factorize(damped(gram_in)), factorize(damped(gram_out)))


def solution(mesh):
    return jax.shard_map(
        local,
        mesh=mesh,
        in_specs=(P("dp", "owner"), P("dp", "owner"), P("dp", None), P("dp", None, None)),
        out_specs=(P("owner", None), P("owner", None)),
        check_vma=False,
    )
```

profile of v0, /device:TPU:29, one launch (start us, length us, event | category | flops | bytes accessed | tf_op | source)
XLA Modules:
  0.0 1959.3 jit_solution(2103061141893019698)
XLA Ops:
  24.9 90.4 %all-reduce.18.cloned.1.call-done = (bf16[256,512]{1,0:T(8,128)(2,1)}, bf16[256,512]{1,0:T(8,128)(2,1)}, bf16[256,512]{1,0:T(8,128)(2,1)}, bf16[256,512]{1,0:T(8...) async-done(((bf16[256,512]{1,0:T(8,128)(2,1)}, bf16[256,512]{1,0:T(8,128)(2,1)}, bf16[256,512]{1,0:T(8,128)(2,1)}, bf16[256,512]{1,0:T(8,128)(2,1)}, ...) | async-done | bytes 1572880 | tf_op jit(solution)/shard_map/psum | solution.py:16
  128.4 50.2 %reduce-scatter.3.cloned.1.call-done = f32[256,1536]{0,1:T(8,128)} async-done(((f32[1024,1536]{0,1:T(8,128)}), f32[256,1536]{0,1:T(8,128)}) %reduce-scatter.3.cloned.1.call-update) | async-done | bytes 1572880 | tf_op jit(solution)/shard_map/reduce_scatter | solution.py:88
  178.6 102.4 %reduce-scatter.5.cloned.1.call-done = f32[512,1536]{0,1:T(8,128)} async-done(((f32[2048,1536]{0,1:T(8,128)}), f32[512,1536]{0,1:T(8,128)}) %reduce-scatter.5.cloned.1.call-update) | async-done | bytes 3145744 | tf_op jit(solution)/shard_map/reduce_scatter | solution.py:89
  281.3 48.0 %all-gather.3.cloned.1.call-done = f32[1024,1536]{0,1:T(8,128)} async-done(((f32[256,1536]{0,1:T(8,128)}), f32[1024,1536]{0,1:T(8,128)}) %all-gather.3.cloned.1.call-update) | async-done | bytes 6291472 | tf_op jit(solution)/shard_map/all_gather | solution.py:92
  337.5 11.7 cholesky.638
  349.4 9.8 custom-call.45
  359.9 11.7 cholesky.657
  371.6 10.1 custom-call.46
  382.4 11.7 cholesky.678
  394.2 9.8 custom-call.47
  404.6 11.9 cholesky.695
  422.8 12.3 select_add_fusion
  438.1 11.7 cholesky.854
  450.0 9.8 custom-call.57
  460.5 12.1 cholesky.873
  473.9 9.8 custom-call.58
  484.4 11.7 cholesky.894
  496.8 9.8 custom-call.59
  507.2 11.9 cholesky.911
  524.1 101.1 %all-reduce.16.cloned.1.call-done = (f32[512,512]{1,0:T(8,128)}, f32[512,512]{1,0:T(8,128)}) async-done(((f32[512,512]{1,0:T(8,128)}, f32[512,512]{1,0:T(8,128)}), (f32[512,512]{1,0:T(8,128)}, f32[512,512]{1,0:T(8,128)})) %all-reduce.16.cloned.1.call-update) | async-done | bytes 2097168 | tf_op jit(solution)/shard_map/psum | solution.py:16
  634.6 39.3 %custom-call.60 = f32[4,128,128]{1,2,0:T(8,128)S(1)} custom-call(f32[4,128,128]{2,1,0:T(8,128)S(1)} %get-tuple-element.122), custom_call_target="InvertDiagBlocksLowerTriangular" | custom-call | tf_op jit(solution)/shard_map/triangular_solve/custom-call.8 | solution.py:58
  696.9 9.3 gather_fusion.5
  717.9 11.7 cholesky.926
  730.2 9.8 custom-call.61
  751.7 39.5 %custom-call.48 = f32[4,128,128]{1,2,0:T(8,128)S(1)} custom-call(f32[4,128,128]{2,1,0:T(8,128)S(1)} %get-tuple-element.119), custom_call_target="InvertDiagBlocksLowerTriangular" | custom-call | tf_op jit(solution)/shard_map/triangular_solve/custom-call.3 | solution.py:58
  822.2 11.7 cholesky.710
  834.5 9.8 custom-call.49
  848.0 12.1 cholesky.945
  861.4 9.8 custom-call.62
  872.8 11.7 cholesky.966
  885.3 9.8 custom-call.63
  896.6 11.9 cholesky.983
  910.3 11.7 cholesky.729
  923.3 9.8 custom-call.50
  935.6 12.1 cholesky.750
  948.3 9.8 custom-call.51
  959.6 11.7 cholesky.767
  993.5 142.4 %all-reduce.14.cloned.1.call-done = (f32[512,1024]{1,0:T(8,128)}, f32[512,1024]{1,0:T(8,128)}) async-done(((f32[512,1024]{1,0:T(8,128)}, f32[512,1024]{1,0:T(8,128)}), (f32[512,1024]{1,0:T(8,128)}, f32[512,1024]{1,0:T(8,128)})) %all-reduce.14.cloned.1.call-update) | async-done | bytes 4194320 | tf_op jit(solution)/shard_map/psum | solution.py:16
  1135.9 11.0 slice_subtract_fusion.1
  1148.2 11.5 while.22
  1160.4 40.3 %custom-call.64 = f32[4,128,128]{1,2,0:T(8,128)S(1)} custom-call(f32[4,128,128]{2,1,0:T(8,128)} %copy-done.60), custom_call_target="InvertDiagBlocksLowerTriangular" | custom-call | tf_op jit(solution)/shard_map/triangular_solve/custom-call.8 | solution.py:58
  1227.0 9.1 gather_fusion.6
  1252.9 11.7 cholesky.998
  1265.2 9.8 custom-call.65
  1290.4 14.0 while.19
  1304.4 40.7 %custom-call.52 = f32[4,128,128]{1,2,0:T(8,128)} custom-call(f32[4,128,128]{2,1,0:T(8,128)} %get-tuple-element.120), custom_call_target="InvertDiagBlocksLowerTriangular" | custom-call | tf_op jit(solution)/shard_map/triangular_solve/custom-call.3 | solution.py:58
  1376.5 11.7 cholesky.782
  1388.9 9.8 custom-call.53
  1403.8 11.9 cholesky.1017
  1417.0 9.8 custom-call.66
  1428.4 11.7 cholesky.1038
  1440.8 9.8 custom-call.67
  1452.6 11.7 cholesky.1055
  1467.9 11.7 cholesky.801
  1482.9 9.8 custom-call.54
  1496.0 11.9 cholesky.822
  1509.2 9.8 custom-call.55
  1521.2 11.7 cholesky.839
  1543.7 211.8 %all-reduce.12.cloned.1.call-done = (f32[512,1536]{1,0:T(8,128)}, f32[512,1536]{1,0:T(8,128)}) async-done(((f32[512,1536]{1,0:T(8,128)}, f32[512,1536]{1,0:T(8,128)}), (f32[512,1536]{1,0:T(8,128)}, f32[512,1536]{1,0:T(8,128)})) %all-reduce.12.cloned.1.call-update) | async-done | bytes 6291472 | tf_op jit(solution)/shard_map/psum | solution.py:16
  1755.6 18.0 slice_subtract_fusion
  1783.2 39.3 %custom-call.68 = f32[4,128,128]{1,2,0:T(8,128)S(1)} custom-call(f32[4,128,128]{2,1,0:T(8,128)S(1)} %get-tuple-element.124), custom_call_target="InvertDiagBlocksLowerTriangular" | custom-call | tf_op jit(solution)/shard_map/triangular_solve/custom-call.8 | solution.py:58
  1831.1 10.1 slice_subtract_fusion.2
  1841.9 13.6 while.20
  1855.6 40.9 %custom-call.56 = f32[4,128,128]{1,2,0:T(8,128)} custom-call(f32[4,128,128]{2,1,0:T(8,128)} %get-tuple-element.121), custom_call_target="InvertDiagBlocksLowerTriangular" | custom-call | tf_op jit(solution)/shard_map/triangular_solve/custom-call.3 | solution.py:58
  (498 shorter events, 435.7 us)
Async XLA Ops:
  7.2 108.1 %all-reduce.18.cloned.1.call-start = ((), (), s32[]{:S(2)}) async-start(), calls=%async_computation.9 | async-start | bytes 3145728 | tf_op jit(solution)/shard_map/psum | solution.py:16
  23.3 1.4 copy-start.63
  24.6 153.9 %reduce-scatter.3.cloned.1.call-start = ((), (), s32[]{:S(2)}) async-start(), calls=%async_computation.2 | async-start | bytes 7864320 | tf_op jit(solution)/shard_map/reduce_scatter | solution.py:88
  120.1 1.1 copy-start.49
  120.2 160.8 %reduce-scatter.5.cloned.1.call-start = ((), (), s32[]{:S(2)}) async-start(), calls=%async_computation.4 | async-start | bytes 15728640 | tf_op jit(solution)/shard_map/reduce_scatter | solution.py:89
  128.4 201.0 %all-gather.3.cloned.1.call-start = ((), (), s32[]{:S(2)}) async-start(), calls=%async_computation.3 | async-start | bytes 7864320 | tf_op jit(solution)/shard_map/all_gather | solution.py:92
  178.6 244.2 %all-gather.5.cloned.1.call-start = ((), (), s32[]{:S(2)}) async-start(), calls=%async_computation.5 | async-start | bytes 15728640 | tf_op jit(solution)/shard_map/all_gather | solution.py:93
  281.0 344.2 %all-reduce.16.cloned.1.call-start = ((), (), s32[]{:S(2)}) async-start(), calls=%async_computation.8 | async-start | bytes 4194304 | tf_op jit(solution)/shard_map/psum | solution.py:16
  333.0 2.7 copy-start.3
  523.3 612.6 %all-reduce.14.cloned.1.call-start = ((), (), s32[]{:S(2)}) async-start(), calls=%async_computation.7 | async-start | bytes 8388608 | tf_op jit(solution)/shard_map/psum | solution.py:16
  524.0 287.1 %copy-start.61 = (pred[1024]{0:T(1024)(128)(4,1)}, pred[1024]{0:T(1024)(128)(4,1)S(1)}, u32[]{:S(2)}) copy-start(pred[1024]{0:T(1024)(128)(4,1)S(1)} %fusion.258) | copy-start | bytes 3076
  634.6 41.6 %copy-start.36 = (f32[512,512]{1,0:T(8,128)}, f32[512,512]{1,0:T(8,128)S(1)}, u32[]{:S(2)}) copy-start(f32[512,512]{1,0:T(8,128)S(1)} %get-tuple-element.612) | copy-start | bytes 3145732
  689.3 7.6 copy-start
  711.2 2.0 copy-start.2
  716.6 27.0 %copy-start.1 = (f32[512,512]{1,0:T(8,128)S(1)}, f32[512,512]{1,0:T(8,128)}, u32[]{:S(2)}) copy-start(f32[512,512]{1,0:T(8,128)} %get-tuple-element.177) | copy-start | bytes 3145732
  791.2 1.8 copy-start.52
  795.7 8.7 copy-start.25
  795.7 4.7 copy-start.53
  797.9 3.5 copy-start.26
  801.4 3.0 copy-start.33
  814.6 33.3 %copy-start.4 = (f32[1024,512]{1,0:T(8,128)}, f32[1024,512]{1,0:T(8,128)S(1)}, u32[]{:S(2)}) copy-start(f32[1024,512]{1,0:T(8,128)S(1)} %fusion.43) | copy-start | bytes 6291460
  822.2 25.7 %copy-start.57 = (f32[128,128]{1,0:T(8,128)S(1)}, f32[128,128]{1,0:T(8,128)}, u32[]{:S(2)}) copy-start(f32[128,128]{1,0:T(8,128)} %copy-done.56) | copy-start | bytes 196612
  822.2 25.9 %slice-start.3 = ((f32[384,128]{1,0:T(8,128)}), f32[128,128]{1,0:T(8,128)S(1)}, s32[]{:S(2)}) async-start(f32[384,128]{1,0:T(8,128)} %convolution_subtract_fusion.17), calls=%async_computation.13 | async-start | bytes 131072 | tf_op jit(solution)/shard_map/jit(cholesky)/cholesky | solution.py:50
  822.2 49.1 %copy-start.46 = (f32[384,128]{1,0:T(8,128)S(1)}, f32[384,128]{1,0:T(8,128)}, u32[]{:S(2)}) copy-start(f32[384,128]{1,0:T(8,128)} %convolution_subtract_fusion.17) | copy-start | bytes 589828
  860.1 50.1 %slice-start.4 = ((f32[384,128]{1,0:T(8,128)}), f32[128,128]{1,0:T(8,128)S(1)}, s32[]{:S(2)}) async-start(f32[384,128]{1,0:T(8,128)} %convolution_subtract_fusion.20), calls=%async_computation.14 | async-start | bytes 131072 | tf_op jit(solution)/shard_map/jit(cholesky)/cholesky | solution.py:50
  895.3 79.3 %slice-start = ((f32[2048,512]{1,0:T(8,128)}), f32[512,512]{1,0:T(8,128)S(1)}, s32[]{:S(2)}) async-start(f32[2048,512]{1,0:T(8,128)} %copy-done.2), calls=%async_computation.10 | async-start | bytes 2097152 | tf_op jit(solution)/shard_map/slice | solution.py:46
  974.7 4.1 slice-start.1
  980.3 775.3 %all-reduce.12.cloned.1.call-start = ((), (), s32[]{:S(2)}) async-start(), calls=%async_computation.6 | async-start | bytes 12582912 | tf_op jit(solution)/shard_map/psum | solution.py:16
  981.0 9.0 copy-start.5
  1135.9 11.0 copy-start.44
  1212.9 6.2 copy-start.9
  1212.9 6.2 copy-start.8
  1219.1 8.0 copy-start.12
  1276.5 5.4 copy-start.41
  1289.6 64.7 %copy-start.17 = (f32[1024,512]{0,1:T(8,128)S(1)}, f32[1024,512]{0,1:T(8,128)}, u32[]{:S(2)}) copy-start(f32[1024,512]{0,1:T(8,128)} %slice_subtract_fusion.3) | copy-start | bytes 6291460
  1352.2 4.6 copy-start.51
  1352.2 5.6 copy-start.23
  1354.3 8.2 copy-start.24
  1357.8 4.7 copy-start.32
  1362.5 3.5 copy-start.62
  1376.5 23.9 %copy-start.40 = (f32[512,512]{1,0:T(8,128)}, f32[512,512]{1,0:T(8,128)S(1)}, u32[]{:S(2)}) copy-start(f32[512,512]{1,0:T(8,128)S(1)} %fusion.110) | copy-start | bytes 3145732
  1376.5 27.1 %copy-start.55 = (f32[128,128]{1,0:T(8,128)S(1)}, f32[128,128]{1,0:T(8,128)}, u32[]{:S(2)}) copy-start(f32[128,128]{1,0:T(8,128)} %copy-done.54) | copy-start | bytes 196612
  1399.2 4.5 slice-start.2
  1400.4 16.0 copy-start.64
  1400.4 26.4 %copy-start.45 = (f32[384,128]{1,0:T(8,128)S(1)}, f32[384,128]{1,0:T(8,128)}, u32[]{:S(2)}) copy-start(f32[384,128]{1,0:T(8,128)} %convolution_subtract_fusion.16) | copy-start | bytes 589828
  1450.8 86.1 %copy-start.14 = (f32[512,1024]{1,0:T(8,128)S(1)}, f32[512,1024]{1,0:T(8,128)}, u32[]{:S(2)}) copy-start(f32[512,1024]{1,0:T(8,128)} %slice.601) | copy-start | bytes 6291460
  1536.9 4.6 copy-start.27
  1538.8 2.8 copy-start.15
  1783.2 41.6 %copy-start.35 = (f32[512,512]{1,0:T(8,128)}, f32[512,512]{1,0:T(8,128)S(1)}, u32[]{:S(2)}) copy-start(f32[512,512]{1,0:T(8,128)S(1)} %get-tuple-element.608) | copy-start | bytes 3145732
  1828.4 2.7 copy-start.34
  1906.6 5.8 copy-start.6
  1912.4 8.0 copy-start.11
  1912.4 8.0 copy-start.43
  1912.4 8.0 copy-start.50
  1912.4 9.0 copy-start.16
  1912.4 9.0 copy-start.19
  1921.4 8.2 copy-start.21
  1924.9 2.9 copy-start.30
  1938.6 4.9 copy-start.7
  1943.4 6.3 copy-start.18
  1943.4 6.3 copy-start.20
  1943.5 6.2 copy-start.22
  1943.5 6.2 copy-start.31
  1943.5 6.2 copy-start.42
  (14 other events, 11.7 us)
Sparse Core Ops, SparseCore 0:
  24.8 90.4 all-reduce.17
  120.3 58.2 reduce-scatter.2
  181.9 99.0 reduce-scatter.4
  282.5 46.7 all-gather.2
  330.8 82.1 all-gather.4
  523.4 101.7 all-reduce.15
  980.4 155.5 all-reduce.13
  1543.8 211.7 all-reduce.11
where the time goes:
time: 1970 us; the launch traced here: 1960 us
  other arithmetic  793 us (40%)
  waiting for transfers between devices  746 us (38%)
  matrix products  217 us (11%)
  local copies, waits for them, and re-layouts  171 us (9%)
  between operations  31.4 us (2%)
    psum x4, waiting for transfers between devices, broadcast(): return lax.psum(jnp.where(mine, shard, jnp.zeros_like(shard)), axis)  546 us
    another operation x90, other arithmetic, factorize(): pivot = jnp.linalg.cholesky(pivot_in)  480 us
    another operation x9, other arithmetic, factorize(): lax.linalg.triangular_solve(pivot_got, residual, left_side=False, lower=T...  242 us
    another operation x42, matrix products, factorize(): lax.linalg.triangular_solve(pivot_got, residual, left_side=False, lower=T...  109 us
    reduce_scatter x1, waiting for transfers between devices, local(): lax.psum_scatter(part_out, 'dp', scatter_dimension=0, tiled=True)  102 us
    another operation x85, local copies, waits for them, and re-layouts, factorize(): lax.linalg.triangular_solve(pivot_got, residual, left_side=False, lower=T...  72 us
    reduce_scatter x1, waiting for transfers between devices, local(): lax.psum_scatter(part_in, 'dp', scatter_dimension=0, tiled=True)  50.2 us
    all_gather x1, waiting for transfers between devices, local(): lax.all_gather(share_in, 'dp', axis=0, tiled=True)  48 us
  transfers between devices with their start and end apart: 8, of which 7 were waited for; matrix products, arithmetic and copies ran while one was open for 6% of the time, Pallas kernels for 0%

commit v1 on v0

v1 whole, which is shorter than its diff:
```python
import functools

import jax
import jax.numpy as jnp
from jax import lax
from jax.experimental import pallas as pl
from jax.experimental.pallas import tpu as pltpu
from jax.sharding import PartitionSpec as P

PB = 512
NPAN = 3
SAMP_DOC = 16
DAMPING = 0.1
BLK = 128
TILE = 256
F32 = jnp.float32
BF16 = jnp.bfloat16
AXES = ("dp", "owner")


def split(x):
    hi = x.astype(BF16)
    return hi, (x - hi.astype(F32)).astype(BF16)


def mm(a, b, ca, cb):
    return lax.dot_general(a, b, (((ca,), (cb,)), ((), ())), preferred_element_type=F32)


def mm3(a, b, ca, cb):
    (ah, al), (bh, bl) = a, b
    return mm(ah, bh, ca, cb) + (mm(ah, bl, ca, cb) + mm(al, bh, ca, cb))


def recip(d):
    r = pltpu.reciprocal(d, approx=True)
    return r * (2.0 - d * r)


def factor_block(a):
    lane = lax.broadcasted_iota(jnp.int32, (8, BLK), 1)
    sub = lax.broadcasted_iota(jnp.int32, (8, BLK), 0)
    groups = BLK // 8
    rows_of = [a[8 * g : 8 * g + 8] for g in range(groups)]
    upper, inverse = [], []

    def fill(x):
        return jnp.broadcast_to(x, (8, BLK))

    for g in range(groups):
        top, c0 = rows_of[g], 8 * g
        rr = [fill(top[i : i + 1, :]) for i in range(8)]
        e = {(i, j): fill(rr[i][:, c0 + j : c0 + j + 1]) for i in range(8) for j in range(i + 1)}
        below = range(g + 1, groups)
        col = {(h, j): fill(rows_of[h][:, c0 + j : c0 + j + 1]) for h in below for j in range(8)}
        mult, src = {}, {}
        for k in range(0, 8, 2):
            p, q, r = e[k, k], e[k + 1, k], e[k + 1, k + 1]
            inv = recip(p * r - q * q)
            pi, qi, ri = p * inv, q * inv, r * inv
            at0, at1 = lane == c0 + k, lane == c0 + k + 1
            s0 = jnp.where(at0, 1.0, jnp.where(at1, 0.0, rr[k]))
            s1 = jnp.where(at1, 1.0, jnp.where(at0, 0.0, rr[k + 1]))
            for i in range(k + 2, 8):
                x, y = e[i, k], e[i, k + 1]
                m0, m1 = (x * r - y * q) * inv, (y * p - x * q) * inv
                for j in range(k + 2, i + 1):
                    e[i, j] = e[i, j] - (m0 * e[j, k] + m1 * e[j, k + 1])
                rr[i] = jnp.where(at0 | at1, 0.0, rr[i]) - (m0 * s0 + m1 * s1)
            later = (lane > c0 + k + 1) & (lane < c0 + 8)
            src[k], src[k + 1] = jnp.where(later, 0.0, s0), jnp.where(later, 0.0, s1)
            for h in below:
                x, y = col[h, k], col[h, k + 1]
                m0, m1 = x * ri - y * qi, y * pi - x * qi
                mult[h, k], mult[h, k + 1] = m0, m1
                for j in range(k + 2, 8):
                    col[h, j] = col[h, j] - (m0 * e[j, k] + m1 * e[j, k + 1])
        for h in below:
            acc = jnp.where((lane >= c0) & (lane < c0 + 8), 0.0, rows_of[h])
            for j in range(0, 8, 2):
                acc = acc - (mult[h, j] * src[j] + mult[h, j + 1] * src[j + 1])
            rows_of[h] = acc
        done = scale = None
        for k in range(8):
            if k % 2 == 0:
                d, row = e[k, k], rr[k]
            else:
                t = e[k, k - 1] / e[k - 1, k - 1]
                d = e[k, k] - t * e[k, k - 1]
                before = lane == c0 + k - 1
                row = jnp.where(before, 0.0, rr[k]) - t * jnp.where(before, 1.0, rr[k - 1])
            s = lax.rsqrt(d)
            row = row * s
            done = row if k == 0 else jnp.where(sub == k, row, done)
            scale = s if k == 0 else jnp.where(sub == k, s, scale)
        diag = c0 + sub
        upper.append(jnp.where(lane >= diag, done, 0.0))
        inverse.append(jnp.where(lane < diag, done, jnp.where(lane == diag, scale, 0.0)))
    return jnp.concatenate(upper, 0), jnp.concatenate(inverse, 0)


def panel_kernel(panel, *refs):
    w_ref, weight_ref = refs[:2]
    prev = refs[2 : 2 + 2 * panel]
    vh_ref, vl_ref, l_ref, sw, a, z, y, lq = refs[2 + 2 * panel :]
    samples = w_ref.shape[0]
    chunk = TILE

    @pl.loop(0, samples // chunk)
    def _(i):
        at = pl.ds(pl.multiple_of(i * chunk, chunk), chunk)
        w = w_ref[at, :].astype(F32)
        sw[at, :] = (weight_ref[at, :] * w).astype(BF16)
        y[at, :] = w

    row = lax.broadcasted_iota(jnp.int32, (PB, PB), 0)
    column = lax.broadcasted_iota(jnp.int32, (PB, PB), 1)
    eye = (row == column).astype(F32)
    gram = mm(sw[...], w_ref[...], 0, 0) + mm(w_ref[...], sw[...], 0, 0)
    a[...] = 0.5 * gram + DAMPING * eye
    z[...] = eye
    for q in range(panel):
        vh, vl = prev[2 * q], prev[2 * q + 1]
        lh, ll = split(mm(sw[...], vh[...], 0, 0) + mm(sw[...], vl[...], 0, 0))
        lq[0], lq[1] = lh, ll
        a[...] -= mm3((lh, ll), (lh, ll), 1, 1)

        @pl.loop(0, samples // chunk)
        def _(i):
            at = pl.ds(pl.multiple_of(i * chunk, chunk), chunk)
            y[at, :] -= mm3((vh[at, :], vl[at, :]), (lq[0], lq[1]), 1, 1)

    l_ref[...] = jnp.zeros((PB, PB), F32)

    @pl.loop(0, PB // BLK)
    def _(b):
        at = pl.ds(pl.multiple_of(b * BLK, BLK), BLK)
        upper, inverse = factor_block(a[at, at])
        x = split(inverse)
        below = lax.broadcasted_iota(jnp.int32, (PB, BLK), 0) >= (b + 1) * BLK
        lcol = jnp.where(below, mm3(split(a[:, at]), x, 1, 1), 0.0)
        l_ref[:, at] = lcol
        l_ref[at, at] = upper.T
        lcol = split(lcol)
        a[...] -= mm3(lcol, lcol, 1, 1)
        zb = mm3(x, split(z[at, :]), 1, 0)
        z[...] -= mm3(lcol, split(zb), 1, 0)
        z[at, :] = zb

    zz = split(z[...])
    lq[0], lq[1] = zz

    @pl.loop(0, samples // chunk)
    def _(i):
        at = pl.ds(pl.multiple_of(i * chunk, chunk), chunk)
        v = mm3(split(y[at, :]), (lq[0], lq[1]), 1, 1)
        vh_ref[at, :], vl_ref[at, :] = split(v)


def factor_panel(window, weight, done):
    panel, samples = len(done), window.shape[0]
    vshape = jax.ShapeDtypeStruct((samples, PB), BF16)
    return pl.pallas_call(
        functools.partial(panel_kernel, panel),
        out_shape=(vshape, vshape, jax.ShapeDtypeStruct((PB, PB), F32)),
        scratch_shapes=[
            pltpu.VMEM((samples, PB), BF16),
            pltpu.VMEM((PB, PB), F32),
            pltpu.VMEM((PB, PB), F32),
            pltpu.VMEM((samples, PB), F32),
            pltpu.VMEM((2, PB, PB), BF16),
        ],
        compiler_params=pltpu.CompilerParams(vmem_limit_bytes=48 << 20),
        name=f"factor_panel_{panel}",
    )(window, weight, *[part for v in done for part in v[:2]])


def rows_kernel(pos_ref, s_ref, *refs):
    parts, (out_ref, buf, lbuf, sem) = refs[:-4], refs[-4:]
    own, other = parts[:9], parts[9:]
    step = pl.program_id(0)

    def copies(group):
        made = []
        for p in range(NPAN):
            made.append((group[3 * p], buf.at[p, 0]))
            made.append((group[3 * p + 1], buf.at[p, 1]))
            made.append((group[3 * p + 2], lbuf.at[p]))
        return [pltpu.make_async_copy(s, d, sem.at[i]) for i, (s, d) in enumerate(made)]

    for mine, group in ((1, own), (0, other)):

        @pl.when((step == 0) & (pos_ref[1] == mine))
        def _():
            for copy in copies(group):
                copy.start()
            for copy in copies(group):
                copy.wait()

    first = pos_ref[0] + step * TILE
    for p in range(NPAN):
        cols = slice(p * PB, (p + 1) * PB)

        @pl.when(first >= (p + 1) * PB)
        def _():
            s = s_ref[...]
            out_ref[:, cols] = mm(s, buf[p, 0], 0, 0) + mm(s, buf[p, 1], 0, 0)

        @pl.when((first >= p * PB) & (first < (p + 1) * PB))
        def _():
            at = pl.multiple_of(jnp.clip(first - p * PB, 0, PB - TILE), TILE)
            out_ref[:, cols] = lbuf[p, pl.ds(at, TILE), :]

        @pl.when(first < p * PB)
        def _():
            out_ref[:, cols] = jnp.zeros((TILE, PB), F32)


def factor_rows(scaled, position, own, other):
    samples, height = scaled.shape
    parts = [x for group in (own, other) for v in group for x in v]
    anywhere = pl.BlockSpec(memory_space=pl.ANY)
    return pl.pallas_call(
        rows_kernel,
        grid_spec=pltpu.PrefetchScalarGridSpec(
            num_scalar_prefetch=1,
            grid=(height // TILE,),
            in_specs=[pl.BlockSpec((samples, TILE), lambda i, pos: (0, i))] + [anywhere] * len(parts),
            out_specs=pl.BlockSpec((TILE, NPAN * PB), lambda i, pos: (i, 0)),
            scratch_shapes=[
                pltpu.VMEM((NPAN, 2, samples, PB), BF16),
                pltpu.VMEM((NPAN, PB, PB), F32),
                pltpu.SemaphoreType.DMA((3 * NPAN,)),
            ],
        ),
        out_shape=jax.ShapeDtypeStruct((height, NPAN * PB), F32),
        compiler_params=pltpu.CompilerParams(vmem_limit_bytes=48 << 20),
        name="factor_rows",
    )(position, scaled, *parts)


class Grid:
    def __init__(self, n_dp, n_owner):
        self.ny, self.no = n_dp // 2, n_owner
        self.nz = 4 if n_owner % 4 == 0 else 1
        self.nx = n_owner // self.nz
        dp, owner = lax.axis_index("dp"), lax.axis_index("owner")
        self.y, self.core = dp // 2, dp % 2
        self.z, self.x = owner // self.nx, owner % self.nx

    def at(self, y, core, z, x):
        return (2 * y + core) * self.no + z * self.nx + x

    def everywhere(self):
        return [
            (y, c, z, x)
            for y in range(self.ny)
            for c in range(2)
            for z in range(self.nz)
            for x in range(self.nx)
        ]

    def send(self, value, moves):
        return lax.ppermute(value, AXES, [(self.at(*a), self.at(*b)) for a, b in moves])

    def other_core(self, value):
        return self.send(value, [((y, c, z, x), (y, 1 - c, z, x)) for y, c, z, x in self.everywhere()])

    def by_core(self, pair):
        return jnp.where(self.core == 0, pair[0], pair[1])

    def gather(self, value, size, index, move):
        parts = [value]
        for k in range(1, size):
            parts.append(self.send(value, move(k)))
        if size == 2:
            swapped = index == 1
            return jnp.concatenate(
                [jnp.where(swapped, parts[1], parts[0]), jnp.where(swapped, parts[0], parts[1])], 0
            )
        rows = value.shape[0]
        both = jnp.concatenate(parts + parts, 0)
        start = ((size - index) % size) * rows
        return lax.dynamic_slice_in_dim(both, start, size * rows, 0)

    def gather_x(self, value):
        return self.gather(
            value,
            self.nx,
            self.x,
            lambda k: [((y, c, z, (x + k) % self.nx), (y, c, z, x)) for y, c, z, x in self.everywhere()],
        )

    def gather_y(self, value):
        return self.gather(
            value,
            self.ny,
            self.y,
            lambda k: [(((y + k) % self.ny, c, z, x), (y, c, z, x)) for y, c, z, x in self.everywhere()],
        )


def spread_window(grid, pieces, roots):
    ny, nz, nx = grid.ny, grid.nz, grid.nx
    keep, give = grid.by_core(pieces), grid.by_core(pieces[::-1])
    got = grid.send(
        give,
        [((y, c, *divmod(roots[1 - c], nx)), (y, 1 - c, *divmod(roots[1 - c], nx))) for y in range(ny) for c in range(2)],
    )
    low = grid.core == 0
    whole = jnp.concatenate([jnp.where(low, keep, got), jnp.where(low, got, keep)], 0)
    rows = whole.shape[0] // nx
    zr = [r // nx for r in roots]
    xr = [r % nx for r in roots]
    root_x = jnp.where(low, xr[0], xr[1])
    root_z = jnp.where(low, zr[0], zr[1])
    part = lax.dynamic_slice_in_dim(whole, grid.x * rows, rows, 0)
    for k in range(1, nx):
        piece = lax.dynamic_slice_in_dim(whole, ((root_x + k) % nx) * rows, rows, 0)
        got = grid.send(
            piece,
            [((y, c, zr[c], xr[c]), (y, c, zr[c], (xr[c] + k) % nx)) for y in range(ny) for c in range(2)],
        )
        part = jnp.where((grid.x - root_x + nx) % nx == k, got, part)
    mine = part
    for k in range(1, nz):
        got = grid.send(
            mine,
            [
                ((y, c, zr[c], x), (y, c, (zr[c] + k) % nz, x))
                for y in range(ny)
                for c in range(2)
                for x in range(nx)
            ],
        )
        part = jnp.where((grid.z - root_z + nz) % nz == k, got, part)
    return grid.gather_y(grid.gather_x(part))


def local(activations, ffn_grads, lengths, sample_pos):
    n_dp, n_owner = lax.axis_size("dp"), lax.axis_size("owner")
    tokens = activations.shape[0]
    total = tokens * n_dp
    grid = Grid(n_dp, n_owner)
    doc_len = lengths[0]
    doc_start = jnp.cumsum(doc_len) - doc_len
    row_index = (doc_start[:, None] + jnp.remainder(sample_pos[0], doc_len[:, None])).reshape(-1)

    def weights(lens):
        scale = lens.astype(F32) / (SAMP_DOC * total)
        return jnp.broadcast_to(scale[..., None], (*lens.shape, SAMP_DOC)).reshape(-1, 1)

    weight = weights(doc_len)
    every_weight = weights(lax.all_gather(doc_len, "dp"))
    hot = (row_index[:, None] == jnp.arange(tokens, dtype=jnp.int32)[None, :]).astype(BF16)
    sampled = [jnp.dot(hot, v, preferred_element_type=F32).astype(BF16) for v in (activations, ffn_grads)]
    scaled = [(weight * s.astype(F32)).astype(BF16) for s in sampled]

    windows = []
    for panel in range(NPAN):
        first = panel * PB
        roots = [first // s.shape[1] for s in sampled]
        pieces = [s[:, first % s.shape[1] : first % s.shape[1] + PB] for s in sampled]
        windows.append(spread_window(grid, pieces, roots))

    own, other = [], []
    for panel in range(NPAN):
        done = factor_panel(windows[panel], every_weight, own)
        own.append(done)
        other.append([grid.other_core(x) for x in done])

    rows = jnp.concatenate(scaled, axis=1)
    rows = grid.gather_y(grid.gather(rows, 2, grid.core, lambda k: [((y, 1 - c, z, x), (y, c, z, x)) for y, c, z, x in grid.everywhere()]))
    width = scaled[0].shape[1]
    every = [rows[:, :width], rows[:, width:]]
    outs = []
    for m in range(2):
        height = every[m].shape[1]
        position = jnp.stack([lax.axis_index("owner") * height, (grid.core == m).astype(jnp.int32)])
        outs.append(factor_rows(every[m], position.astype(jnp.int32), own, other))
    return tuple(outs)


def solution(mesh):
    return jax.shard_map(
        local,
        mesh=mesh,
        in_specs=(P("dp", "owner"), P("dp", "owner"), P("dp", None), P("dp", None, None)),
        out_specs=(P("owner", None), P("owner", None)),
        check_vma=False,
    )
```

time: 1970 us -> 332 us (0.17)
  other arithmetic: 793 us -> 22.6 us
  waiting for transfers between devices: 746 us -> 102 us
  matrix products: 217 us -> 9.43 us
  local copies, waits for them, and re-layouts: 171 us -> 8.33 us
  Pallas kernels: 0 us -> 143 us
  starting transfers between devices: 0.54 us -> 33.3 us
  between operations: 31.4 us -> 1.7 us
    another operation x103 -> x3, other arithmetic: 723 us -> 0.23 us  [the longest x90 480 us: factorize(): pivot = jnp.linalg.cholesky(pivot_in)]
    psum x4 -> x0, waiting for transfers between devices: 546 us -> none  [broadcast(): return lax.psum(jnp.where(mine, shard, jnp.zeros_like(shard)), axis)]
    reduce_scatter x2 -> x0, waiting for transfers between devices: 153 us -> none  [the longest x1 102 us: local(): lax.psum_scatter(part_out, 'dp', scatter_dimension=0, tiled=True)]
    pallas_call x0 -> x5, Pallas kernels: none -> 143 us  [the longest x3 104 us: factor_panel(): pl.pallas_call(functools.partial(panel_kernel, panel), out_shape=(vshape,...]
    another operation x78 -> x0, matrix products: 141 us -> none  [the longest x42 109 us: factorize(): lax.linalg.triangular_solve(pivot_got, residual, left_side=False, lower=T...]
    ppermute x0 -> x32, waiting for transfers between devices: none -> 102 us  [send(): lax.ppermute(value, AXES, [(self.at(*a), self.at(*b)) for a, b in moves])]
    another operation x121 -> x1, local copies, waits for them, and re-layouts: 78.3 us -> 0.74 us  [the longest x85 72 us: factorize(): lax.linalg.triangular_solve(pivot_got, residual, left_side=False, lower=T...]
    dot_general x10 -> x2, matrix products: 76.4 us -> 9.43 us  [local(): jnp.dot(hot, v, preferred_element_type=F32).astype(BF16)]
  transfers between devices with their start and end apart: 8 -> 32, of which waited for: 7 -> 6; matrix products, arithmetic and copies ran while one was open for 6% -> 6% of each run, Pallas kernels for 0% -> 32%
where the time goes in v1:
time: 332 us; the launch traced here: 325 us
  Pallas kernels  143 us (43%)
  waiting for transfers between devices  102 us (31%)
  starting transfers between devices  33.3 us (10%)
  other arithmetic  22.6 us (7%)
  matrix products  9.43 us (3%)
  local copies, waits for them, and re-layouts  8.33 us (3%)
  blocking collectives  4.82 us (1%)
    pallas_call x3, Pallas kernels, factor_panel(): pl.pallas_call(functools.partial(panel_kernel, panel), out_shape=(vshape,...  104 us
    ppermute x32, waiting for transfers between devices, send(): lax.ppermute(value, AXES, [(self.at(*a), self.at(*b)) for a, b in moves])  102 us
    pallas_call x2, Pallas kernels, factor_rows(): pl.pallas_call(rows_kernel, grid_spec=pltpu.PrefetchScalarGridSpec(num_sc...  39.1 us
    ppermute x32, starting transfers between devices, send(): lax.ppermute(value, AXES, [(self.at(*a), self.at(*b)) for a, b in moves])  33.3 us
    dot_general x2, matrix products, local(): jnp.dot(hot, v, preferred_element_type=F32).astype(BF16)  9.43 us
    select_n x8, other arithmetic, gather(): jnp.where(swapped, parts[1], parts[0])  6.99 us
  transfers between devices with their start and end apart: 32, of which 6 were waited for; matrix products, arithmetic and copies ran while one was open for 6% of the time, Pallas kernels for 32%

profile of v1, /device:TPU:29, one launch (start us, length us, event | category | flops | bytes accessed | tf_op | source)
XLA Modules:
  0.0 325.4 jit_solution(2917091596657071423)
XLA Ops:
  0.6 0.7 broadcast_compare_fusion
  1.3 0.7 fusion.12
  2.0 0.8 squeeze.7
  3.1 0.7 copy.11
  4.0 0.7 compare_select_fusion
  5.1 3.5 %multiply_convert_fusion.1 = (bf16[256,1024]{1,0:T(8,128)(2,1)S(1)}, bf16[256,1024]{1,0:T(8,128)(2,1)S(1)}) fusion(f32[256]{0:T(256)S(1)} %mul.35, bf16[2048,1024]{1,0:T(8,128)(2,1)} %param.4, s32[256]{0:T(256)S(1)} %fusion.11), kind=kOutput, calls=%fused_computation.16 | convolution fusion | flops 1075314688 | bytes 5244928 | tf_op jit(solution)/shard_map/dot_general | solution.py:356
  8.6 6.0 %multiply_convert_fusion = (bf16[256,2048]{1,0:T(8,128)(2,1)S(1)}, bf16[256,2048]{1,0:T(8,128)(2,1)S(1)}) fusion(f32[256]{0:T(256)S(1)} %mul.35, bf16[2048,2048]{1,0:T(8,128)(2,1)} %param.5, s32[256]{0:T(256)S(1)} %fusion.11), kind=kOutput, calls=%fused_computation.6 | convolution fusion | flops 2150105088 | bytes 10487808 | tf_op jit(solution)/shard_map/dot_general | solution.py:356
  14.6 0.7 collective-permute-start.16
  15.3 1.4 collective-permute-start.2
  16.7 0.7 copy-done.18
  17.4 2.1 broadcast_select_fusion.10
  19.5 0.3 fusion.10
  19.8 1.4 collective-permute-start.17
  21.2 1.3 collective-permute-start.9
  22.5 1.3 pad_maximum_fusion.3
  23.8 0.7 collective-permute-start
  24.5 4.8 %all-gather = s32[4,1,16]{2,1,0:T(1,128)S(1)} all-gather(s32[1,1,16]{2,1,0:T(1,128)S(1)} %bitcast.19), channel_id=1, replica_groups=mesh['dp'=4,'owner'=8] {'dp'}, dimensions={0}, use_global_device_ids=true | all-gather | bytes 320 | tf_op jit(solution)/shard_map/all_gather | solution.py:354
  29.3 1.4 collective-permute-start.3
  30.7 0.4 fusion.9
  31.1 1.4 collective-permute-start.20
  32.4 1.4 collective-permute-start.19
  33.8 1.1 broadcast_select_fusion.14
  34.9 0.7 collective-permute-start.10
  35.7 0.3 reshape.113.refs_1_
  36.0 1.3 collective-permute-start.18
  37.3 1.2 fusion.7
  38.5 0.7 collective-permute-start.6
  39.2 0.7 collective-permute-start.5
  39.9 1.3 collective-permute-start.4
  41.2 0.4 fusion.5
  41.6 13.9 %collective-permute-done.18 = bf16[256,512]{1,0:T(8,128)(2,1)S(1)} collective-permute-done((bf16[256,512]{1,0:T(8,128)(2,1)S(1)}, bf16[256,512]{1,0:T(8,128)(2,1)S(1)}, u32[]{:S(2)}, u32[]{:S(2)}) %collective-permute-start.18) | collective-permute-done | bytes 262176 | tf_op jit(solution)/shard_map/ppermute | solution.py:264
  55.5 0.7 collective-permute-start.13
  56.3 0.7 collective-permute-start.12
  57.0 1.5 collective-permute-start.11
  58.4 13.9 %collective-permute-done.4 = bf16[256,512]{1,0:T(8,128)(2,1)S(1)} collective-permute-done((bf16[256,512]{1,0:T(8,128)(2,1)S(1)}, bf16[256,512]{1,0:T(8,128)(2,1)S(1)}, u32[]{:S(2)}, u32[]{:S(2)}) %collective-permute-start.4) | collective-permute-done | bytes 262176 | tf_op jit(solution)/shard_map/ppermute | solution.py:264
  72.3 1.0 collective-permute-start.21
  73.4 0.6 collective-permute-start.7
  74.0 2.1 broadcast_select_fusion.3
  76.1 2.0 pad_maximum_fusion.1
  78.3 0.5 copy-done.11
  79.0 10.2 %collective-permute-done.11 = bf16[256,512]{1,0:T(8,128)(2,1)S(1)} collective-permute-done((bf16[256,512]{1,0:T(8,128)(2,1)S(1)}, bf16[256,512]{1,0:T(8,128)(2,1)S(1)}, u32[]{:S(2)}, u32[]{:S(2)}) %collective-permute-start.11) | collective-permute-done | bytes 262176 | tf_op jit(solution)/shard_map/ppermute | solution.py:264
  89.3 0.5 collective-permute-start.14
  90.2 5.0 %collective-permute-done.14 = bf16[256,512]{1,0:T(8,128)(2,1)S(1)} collective-permute-done((bf16[256,512]{1,0:T(8,128)(2,1)S(1)}, bf16[256,512]{1,0:T(8,128)(2,1)S(1)}, u32[]{:S(2)}, u32[]{:S(2)}) %collective-permute-start.14) | collective-permute-done | bytes 262176 | tf_op jit(solution)/shard_map/ppermute | solution.py:264
  95.5 1.3 collective-permute-start.22
  96.9 58.6 %collective-permute-done.8 = bf16[512,512]{1,0:T(8,128)(2,1)S(1)} collective-permute-done((bf16[512,512]{1,0:T(8,128)(2,1)S(1)}, bf16[512,512]{1,0:T(8,128)(2,1)S(1)}, u32[]{:S(2)}, u32[]{:S(2)}) %collective-permute-start.8) | collective-permute-done | bytes 524320 | tf_op jit(solution)/shard_map/ppermute | solution.py:264
  155.8 29.2 %factor_panel_0.1 = (bf16[1024,512]{1,0:T(8,128)(2,1)S(1)}, bf16[1024,512]{1,0:T(8,128)(2,1)S(1)}, f32[512,512]{1,0:T(8,128)}) custom-call(bf16[1024,512]{1,0:T(8,128)(2,1)S(1)} %pad_maximum_fusion.4.refs_0_, f32[1024,1]{1,0:T(8,128)S(1)} %reshape.113.refs_1_), custom_call_target="tpu_custom_call" | custom-call | tf_op jit(solution)/shard_map/factor_panel_0/pallas_call | solution.py:163
  184.9 10.1 %collective-permute-start.25 = (f32[512,512]{1,0:T(8,128)}, f32[512,512]{1,0:T(8,128)}, u32[]{:S(2)}, u32[]{:S(2)}) collective-permute-start(f32[512,512]{1,0:T(8,128)} %get-tuple-element.13.refs_2_), channel_id=1, source_target_pairs={{0,8},{1,9},{2,10},{3,11},{4,12},{5,13},{6,14},{7,15},{8,0},{9,1},... | collective-permute-start | bytes 3145736 | tf_op jit(solution)/shard_map/ppermute | solution.py:264
  195.0 0.5 collective-permute-start.24
  195.8 35.1 %factor_panel_1.1 = (bf16[1024,512]{1,0:T(8,128)(2,1)S(1)}, bf16[1024,512]{1,0:T(8,128)(2,1)S(1)}, f32[512,512]{1,0:T(8,128)}) custom-call(bf16[1024,512]{1,0:T(8,128)(2,1)S(1)} %pad_maximum_fusion.5.refs_0_, f32[1024,1]{1,0:T(8,128)S(1)} %reshape.113.refs_1_, bf16[1024,512]{1,0:T(8,128)(2,1)S(1)} %get-tuple-element.11.refs_2_.refs_0_, bf16[1024,512]{1,0:T(8,128)(2,1)} %copy-done), custom_call_target="tpu_custom_call" | custom-call | tf_op jit(solution)/shard_map/factor_panel_1/pallas_call | solution.py:163
  230.9 1.0 copy-done.2
  231.8 1.0 copy-done.4
  233.1 1.2 broadcast_select_fusion.5
  234.4 40.2 %factor_panel_2.1 = (bf16[1024,512]{1,0:T(8,128)(2,1)S(1)}, bf16[1024,512]{1,0:T(8,128)(2,1)S(1)}, f32[512,512]{1,0:T(8,128)S(1)}) custom-call(bf16[1024,512]{1,0:T(8,128)(2,1)S(1)} %pad_maximum_fusion.6.refs_0_, f32[1024,1]{1,0:T(8,128)S(1)} %reshape.113.refs_1_, bf16[1024,512]{1,0:T(8,128)(2,1)S(1)} %get-tuple-element.11.refs_2_.refs_0_, ...), custom_call_target="tpu_custom_call" | custom-call | tf_op jit(solution)/shard_map/factor_panel_2/pallas_call | solution.py:163
  274.7 0.4 collective-permute-start.26
  275.3 0.3 collective-permute-start.29
  275.8 0.3 collective-permute-start.31
  276.1 3.2 broadcast_select_fusion.1
  279.3 1.5 pad_maximum_fusion.2.s_ref
  280.8 2.4 pad_maximum_fusion.s_ref
  283.4 1.1 copy-done.12
  284.5 0.3 copy-done.13
  284.9 1.0 copy-done.16
  285.8 15.5 %factor_rows.2 = f32[1024,1536]{1,0:T(8,128)} custom-call(s32[2]{0:T(128)S(1)} %get-tuple-element.53.pos_ref, bf16[1024,1024]{1,0:T(8,128)(2,1)} %pad_maximum_fusion.2.s_ref, bf16[1024,512]{1,0:T(8,128)(2,1)S(1)} %get-tuple-element.11.refs_2_.refs_0_, bf16[1024,512]{1,0:T(8,128)(2,1)S(1)} %copy-done.1, f32[512,512]{1,0:T(8,128)} %get-tuple-element.13.refs_2_, ...), custom_call_target="tpu_custom_call" | custom-call | tf_op jit(solution)/shard_map/factor_rows/pallas_call | solution.py:223
  301.4 23.5 %factor_rows.3 = f32[2048,1536]{1,0:T(8,128)} custom-call(s32[2]{0:T(128)S(1)} %get-tuple-element.54.pos_ref, bf16[1024,2048]{1,0:T(8,128)(2,1)} %pad_maximum_fusion.s_ref, bf16[1024,512]{1,0:T(8,128)(2,1)S(1)} %get-tuple-element.11.refs_2_.refs_0_, bf16[1024,512]{1,0:T(8,128)(2,1)S(1)} %copy-done.1, f32[512,512]{1,0:T(8,128)} %get-tuple-element.13.refs_2_, ...), custom_call_target="tpu_custom_call" | custom-call | tf_op jit(solution)/shard_map/factor_rows/pallas_call | solution.py:223
  (96 shorter events, 3.8 us)
Async XLA Ops:
  8.5 6.0 %copy-start.17 = (bf16[256,1024]{1,0:T(8,128)(2,1)}, bf16[256,1024]{1,0:T(8,128)(2,1)S(1)}, u32[]{:S(2)}) copy-start(bf16[256,1024]{1,0:T(8,128)(2,1)S(1)} %get-tuple-element.52) | copy-start | bytes 1572868
  14.6 2.1 collective-permute-start.16
  15.3 2.1 collective-permute-start.2
  16.6 7.8 %copy-start.19 = (s32[1,16]{1,0:T(1,128)S(1)}, s32[1,16]{1,0:T(1,128)}, u32[]{:S(2)}) copy-start(s32[1,16]{1,0:T(1,128)} %param.6) | copy-start | bytes 196
  16.7 0.7 copy-start.18
  19.8 10.9 %collective-permute-start.17 = (bf16[256,512]{1,0:T(8,128)(2,1)S(1)}, bf16[256,512]{1,0:T(8,128)(2,1)}, u32[]{:S(2)}, u32[]{:S(2)}) collective-permute-start(bf16[256,512]{1,0:T(8,128)(2,1)S(1)} %fusion.10), channel_id=1, source_target_pairs={{1,0},{8,9},{17,16},{24,25}} | collective-permute-start | bytes 786440 | tf_op jit(solution)/shard_map/ppermute | solution.py:264
  21.2 12.6 %collective-permute-start.9 = (bf16[256,512]{1,0:T(8,128)(2,1)}, bf16[256,512]{1,0:T(8,128)(2,1)}, u32[]{:S(2)}, u32[]{:S(2)}) collective-permute-start(bf16[256,512]{1,0:T(8,128)(2,1)} %get-tuple-element.30), channel_id=1, source_target_pairs={{0,8},{8,0},{16,24},{24,16}} | collective-permute-start | bytes 786440 | tf_op jit(solution)/shard_map/ppermute | solution.py:264
  23.8 49.6 %collective-permute-start = (bf16[256,3072]{1,0:T(8,128)(2,1)}, bf16[256,3072]{1,0:T(8,128)(2,1)}, u32[]{:S(2)}, u32[]{:S(2)}) collective-permute-start(bf16[256,3072]{1,0:T(8,128)(2,1)} %pad_maximum_fusion.3), channel_id=1, source_target_pairs={{8,0},{9,1},{10,2},{11,3},{12,4},{13,5},{14,6},{15,7},{0,8},{1,9},... | collective-permute-start | bytes 4718600 | tf_op jit(solution)/shard_map/ppermute | solution.py:264
  29.3 6.7 %collective-permute-start.3 = (bf16[256,512]{1,0:T(8,128)(2,1)}, bf16[256,512]{1,0:T(8,128)(2,1)}, u32[]{:S(2)}, u32[]{:S(2)}) collective-permute-start(bf16[256,512]{1,0:T(8,128)(2,1)} %get-tuple-element.31), channel_id=1, source_target_pairs={{0,1},{8,9},{16,17},{24,25}} | collective-permute-start | bytes 786440 | tf_op jit(solution)/shard_map/ppermute | solution.py:264
  31.1 7.4 %collective-permute-start.20 = (bf16[256,512]{1,0:T(8,128)(2,1)S(1)}, bf16[256,512]{1,0:T(8,128)(2,1)}, u32[]{:S(2)}, u32[]{:S(2)}) collective-permute-start(bf16[256,512]{1,0:T(8,128)(2,1)S(1)} %fusion.9), channel_id=1, source_target_pairs={{0,2},{1,3},{8,10},{9,11},{16,18},{17,19},{24,26},{25,27}} | collective-permute-start | bytes 786440 | tf_op jit(solution)/shard_map/ppermute | solution.py:264
  32.4 6.8 %collective-permute-start.19 = (bf16[256,512]{1,0:T(8,128)(2,1)S(1)}, bf16[256,512]{1,0:T(8,128)(2,1)}, u32[]{:S(2)}, u32[]{:S(2)}) collective-permute-start(bf16[256,512]{1,0:T(8,128)(2,1)S(1)} %fusion.9), channel_id=1, source_target_pairs={{0,4},{1,5},{8,12},{9,13},{16,20},{17,21},{24,28},{25,29}} | collective-permute-start | bytes 786440 | tf_op jit(solution)/shard_map/ppermute | solution.py:264
  34.9 5.0 %collective-permute-start.10 = (bf16[256,512]{1,0:T(8,128)(2,1)S(1)}, bf16[256,512]{1,0:T(8,128)(2,1)S(1)}, u32[]{:S(2)}, u32[]{:S(2)}) collective-permute-start(bf16[256,512]{1,0:T(8,128)(2,1)S(1)} %get-tuple-element.27), channel_id=1, source_target_pairs={{0,1},{8,9},{16,17},{24,25}} | collective-permute-start | bytes 786440 | tf_op jit(solution)/shard_map/ppermute | solution.py:264
  36.0 19.5 %collective-permute-start.18 = (bf16[256,512]{1,0:T(8,128)(2,1)S(1)}, bf16[256,512]{1,0:T(8,128)(2,1)S(1)}, u32[]{:S(2)}, u32[]{:S(2)}) collective-permute-start(bf16[256,512]{1,0:T(8,128)(2,1)S(1)} %fusion.9), channel_id=1, source_target_pairs={{0,6},{1,7},{8,14},{9,15},{16,22},{17,23},{24,30},{25,31}} | collective-permute-start | bytes 786440 | tf_op jit(solution)/shard_map/ppermute | solution.py:264
  38.5 17.7 %collective-permute-start.6 = (bf16[256,512]{1,0:T(8,128)(2,1)S(1)}, bf16[256,512]{1,0:T(8,128)(2,1)S(1)}, u32[]{:S(2)}, u32[]{:S(2)}) collective-permute-start(bf16[256,512]{1,0:T(8,128)(2,1)S(1)} %fusion.7), channel_id=1, source_target_pairs={{0,2},{1,3},{8,10},{9,11},{16,18},{17,19},{24,26},{25,27}} | collective-permute-start | bytes 786440 | tf_op jit(solution)/shard_map/ppermute | solution.py:264
  39.2 17.7 %collective-permute-start.5 = (bf16[256,512]{1,0:T(8,128)(2,1)S(1)}, bf16[256,512]{1,0:T(8,128)(2,1)S(1)}, u32[]{:S(2)}, u32[]{:S(2)}) collective-permute-start(bf16[256,512]{1,0:T(8,128)(2,1)S(1)} %fusion.7), channel_id=1, source_target_pairs={{0,4},{1,5},{8,12},{9,13},{16,20},{17,21},{24,28},{25,29}} | collective-permute-start | bytes 786440 | tf_op jit(solution)/shard_map/ppermute | solution.py:264
  39.9 32.4 %collective-permute-start.4 = (bf16[256,512]{1,0:T(8,128)(2,1)S(1)}, bf16[256,512]{1,0:T(8,128)(2,1)S(1)}, u32[]{:S(2)}, u32[]{:S(2)}) collective-permute-start(bf16[256,512]{1,0:T(8,128)(2,1)S(1)} %fusion.7), channel_id=1, source_target_pairs={{0,6},{1,7},{8,14},{9,15},{16,22},{17,23},{24,30},{25,31}} | collective-permute-start | bytes 786440 | tf_op jit(solution)/shard_map/ppermute | solution.py:264
  55.5 23.3 %collective-permute-start.13 = (bf16[256,512]{1,0:T(8,128)(2,1)S(1)}, bf16[256,512]{1,0:T(8,128)(2,1)S(1)}, u32[]{:S(2)}, u32[]{:S(2)}) collective-permute-start(bf16[256,512]{1,0:T(8,128)(2,1)S(1)} %fusion.5), channel_id=1, source_target_pairs={{0,2},{1,3},{8,10},{9,11},{16,18},{17,19},{24,26},{25,27}} | collective-permute-start | bytes 786440 | tf_op jit(solution)/shard_map/ppermute | solution.py:264
  56.3 22.7 %collective-permute-start.12 = (bf16[256,512]{1,0:T(8,128)(2,1)S(1)}, bf16[256,512]{1,0:T(8,128)(2,1)S(1)}, u32[]{:S(2)}, u32[]{:S(2)}) collective-permute-start(bf16[256,512]{1,0:T(8,128)(2,1)S(1)} %fusion.5), channel_id=1, source_target_pairs={{0,4},{1,5},{8,12},{9,13},{16,20},{17,21},{24,28},{25,29}} | collective-permute-start | bytes 786440 | tf_op jit(solution)/shard_map/ppermute | solution.py:264
  57.0 32.2 %collective-permute-start.11 = (bf16[256,512]{1,0:T(8,128)(2,1)S(1)}, bf16[256,512]{1,0:T(8,128)(2,1)S(1)}, u32[]{:S(2)}, u32[]{:S(2)}) collective-permute-start(bf16[256,512]{1,0:T(8,128)(2,1)S(1)} %fusion.5), channel_id=1, source_target_pairs={{0,6},{1,7},{8,14},{9,15},{16,22},{17,23},{24,30},{25,31}} | collective-permute-start | bytes 786440 | tf_op jit(solution)/shard_map/ppermute | solution.py:264
  72.3 17.8 %collective-permute-start.21 = (bf16[256,512]{1,0:T(8,128)(2,1)S(1)}, bf16[256,512]{1,0:T(8,128)(2,1)S(1)}, u32[]{:S(2)}, u32[]{:S(2)}) collective-permute-start(bf16[256,512]{1,0:T(8,128)(2,1)S(1)} %select_select_fusion), channel_id=1, source_target_pairs={{1,0},{0,1},{3,2},{2,3},{5,4},{4,5},{7,6},{6,7},{9,8},{8,9},{11,10... | collective-permute-start | bytes 786440 | tf_op jit(solution)/shard_map/ppermute | solution.py:264
  73.4 16.4 %collective-permute-start.7 = (bf16[256,512]{1,0:T(8,128)(2,1)S(1)}, bf16[256,512]{1,0:T(8,128)(2,1)S(1)}, u32[]{:S(2)}, u32[]{:S(2)}) collective-permute-start(bf16[256,512]{1,0:T(8,128)(2,1)S(1)} %select_select_fusion.2), channel_id=1, source_target_pairs={{1,0},{0,1},{3,2},{2,3},{5,4},{4,5},{7,6},{6,7},{9,8},{8,9},{11,10... | collective-permute-start | bytes 786440 | tf_op jit(solution)/shard_map/ppermute | solution.py:264
  76.1 2.2 copy-start.9
  76.1 2.7 copy-start.11
  78.8 197.0 %collective-permute-start.1 = (bf16[512,3072]{1,0:T(8,128)(2,1)}, bf16[512,3072]{1,0:T(8,128)(2,1)}, u32[]{:S(2)}, u32[]{:S(2)}) collective-permute-start(bf16[512,3072]{1,0:T(8,128)(2,1)} %pad_maximum_fusion.1), channel_id=1, source_target_pairs={{16,0},{17,1},{18,2},{19,3},{20,4},{21,5},{22,6},{23,7},{24,8},{25... | collective-permute-start | bytes 9437192 | tf_op jit(solution)/shard_map/ppermute | solution.py:264
  89.3 5.9 %collective-permute-start.14 = (bf16[256,512]{1,0:T(8,128)(2,1)S(1)}, bf16[256,512]{1,0:T(8,128)(2,1)S(1)}, u32[]{:S(2)}, u32[]{:S(2)}) collective-permute-start(bf16[256,512]{1,0:T(8,128)(2,1)S(1)} %select_select_fusion.1), channel_id=1, source_target_pairs={{1,0},{0,1},{3,2},{2,3},{5,4},{4,5},{7,6},{6,7},{9,8},{8,9},{11,10... | collective-permute-start | bytes 786440 | tf_op jit(solution)/shard_map/ppermute | solution.py:264
  89.9 65.6 %collective-permute-start.8 = (bf16[512,512]{1,0:T(8,128)(2,1)S(1)}, bf16[512,512]{1,0:T(8,128)(2,1)S(1)}, u32[]{:S(2)}, u32[]{:S(2)}) collective-permute-start(bf16[512,512]{1,0:T(8,128)(2,1)S(1)} %pad_maximum_fusion.7), channel_id=1, source_target_pairs={{16,0},{17,1},{18,2},{19,3},{20,4},{21,5},{22,6},{23,7},{24,8},{25... | collective-permute-start | bytes 1572872 | tf_op jit(solution)/shard_map/ppermute | solution.py:264
  95.2 99.8 %collective-permute-start.15 = (bf16[512,512]{1,0:T(8,128)(2,1)S(1)}, bf16[512,512]{1,0:T(8,128)(2,1)S(1)}, u32[]{:S(2)}, u32[]{:S(2)}) collective-permute-start(bf16[512,512]{1,0:T(8,128)(2,1)S(1)} %pad_maximum_fusion.8), channel_id=1, source_target_pairs={{16,0},{17,1},{18,2},{19,3},{20,4},{21,5},{22,6},{23,7},{24,8},{25... | collective-permute-start | bytes 1572872 | tf_op jit(solution)/shard_map/ppermute | solution.py:264
  95.5 137.3 %collective-permute-start.22 = (bf16[512,512]{1,0:T(8,128)(2,1)S(1)}, bf16[512,512]{1,0:T(8,128)(2,1)}, u32[]{:S(2)}, u32[]{:S(2)}) collective-permute-start(bf16[512,512]{1,0:T(8,128)(2,1)S(1)} %pad_maximum_fusion.9), channel_id=1, source_target_pairs={{16,0},{17,1},{18,2},{19,3},{20,4},{21,5},{22,6},{23,7},{24,8},{25... | collective-permute-start | bytes 1572872 | tf_op jit(solution)/shard_map/ppermute | solution.py:264
  184.9 10.8 %copy-start = (bf16[1024,512]{1,0:T(8,128)(2,1)}, bf16[1024,512]{1,0:T(8,128)(2,1)S(1)}, u32[]{:S(2)}) copy-start(bf16[1024,512]{1,0:T(8,128)(2,1)S(1)} %get-tuple-element.12.refs_3_.refs_1_) | copy-start | bytes 3145732
  184.9 89.7 %collective-permute-start.25 = (f32[512,512]{1,0:T(8,128)}, f32[512,512]{1,0:T(8,128)}, u32[]{:S(2)}, u32[]{:S(2)}) collective-permute-start(f32[512,512]{1,0:T(8,128)} %get-tuple-element.13.refs_2_), channel_id=1, source_target_pairs={{0,8},{1,9},{2,10},{3,11},{4,12},{5,13},{6,14},{7,15},{8,0},{9,1},... | collective-permute-start | bytes 3145736 | tf_op jit(solution)/shard_map/ppermute | solution.py:264
  195.0 80.1 %collective-permute-start.23 = (bf16[1024,512]{1,0:T(8,128)(2,1)S(1)}, bf16[1024,512]{1,0:T(8,128)(2,1)}, u32[]{:S(2)}, u32[]{:S(2)}) collective-permute-start(bf16[1024,512]{1,0:T(8,128)(2,1)S(1)} %get-tuple-element.11.refs_2_.refs_0_), channel_id=1, source_target_pairs={{0,8},{1,9},{2,10},{3,11},{4,12},{5,13},{6,14},{7,15},{8,0},{9,1},... | collective-permute-start | bytes 3145736 | tf_op jit(solution)/shard_map/ppermute | solution.py:264
  195.0 80.3 %collective-permute-start.24 = (bf16[1024,512]{1,0:T(8,128)(2,1)S(1)}, bf16[1024,512]{1,0:T(8,128)(2,1)}, u32[]{:S(2)}, u32[]{:S(2)}) collective-permute-start(bf16[1024,512]{1,0:T(8,128)(2,1)S(1)} %get-tuple-element.12.refs_3_.refs_1_), channel_id=1, source_target_pairs={{0,8},{1,9},{2,10},{3,11},{4,12},{5,13},{6,14},{7,15},{8,0},{9,1},... | collective-permute-start | bytes 3145736 | tf_op jit(solution)/shard_map/ppermute | solution.py:264
  230.9 1.0 copy-start.2
  231.8 1.0 copy-start.4
  232.8 42.8 %collective-permute-start.28 = (f32[512,512]{1,0:T(8,128)}, f32[512,512]{1,0:T(8,128)}, u32[]{:S(2)}, u32[]{:S(2)}) collective-permute-start(f32[512,512]{1,0:T(8,128)} %get-tuple-element.16.refs_5_), channel_id=1, source_target_pairs={{0,8},{1,9},{2,10},{3,11},{4,12},{5,13},{6,14},{7,15},{8,0},{9,1},... | collective-permute-start | bytes 3145736 | tf_op jit(solution)/shard_map/ppermute | solution.py:264
  234.4 40.3 %copy-start.3 = (bf16[1024,512]{1,0:T(8,128)(2,1)S(1)}, bf16[1024,512]{1,0:T(8,128)(2,1)}, u32[]{:S(2)}) copy-start(bf16[1024,512]{1,0:T(8,128)(2,1)} %copy-done.2) | copy-start | bytes 3145732
  234.4 40.6 %copy-start.5 = (bf16[1024,512]{1,0:T(8,128)(2,1)S(1)}, bf16[1024,512]{1,0:T(8,128)(2,1)}, u32[]{:S(2)}) copy-start(bf16[1024,512]{1,0:T(8,128)(2,1)} %copy-done.4) | copy-start | bytes 3145732
  234.4 41.7 %copy-start.10 = (bf16[256,3072]{1,0:T(8,128)(2,1)S(1)}, bf16[256,3072]{1,0:T(8,128)(2,1)}, u32[]{:S(2)}) copy-start(bf16[256,3072]{1,0:T(8,128)(2,1)} %copy-done.9) | copy-start | bytes 4718596
  274.6 4.6 %copy-start.6 = (bf16[1024,512]{1,0:T(8,128)(2,1)}, bf16[1024,512]{1,0:T(8,128)(2,1)S(1)}, u32[]{:S(2)}) copy-start(bf16[1024,512]{1,0:T(8,128)(2,1)S(1)} %get-tuple-element.17.refs_6_) | copy-start | bytes 3145732
  274.6 4.6 %copy-start.7 = (bf16[1024,512]{1,0:T(8,128)(2,1)}, bf16[1024,512]{1,0:T(8,128)(2,1)S(1)}, u32[]{:S(2)}) copy-start(bf16[1024,512]{1,0:T(8,128)(2,1)S(1)} %get-tuple-element.18.refs_7_) | copy-start | bytes 3145732
  274.6 4.6 %copy-start.8 = (f32[512,512]{1,0:T(8,128)}, f32[512,512]{1,0:T(8,128)S(1)}, u32[]{:S(2)}) copy-start(f32[512,512]{1,0:T(8,128)S(1)} %get-tuple-element.19.refs_8_) | copy-start | bytes 3145732
  274.7 8.5 %collective-permute-start.26 = (bf16[1024,512]{1,0:T(8,128)(2,1)S(1)}, bf16[1024,512]{1,0:T(8,128)(2,1)S(1)}, u32[]{:S(2)}, u32[]{:S(2)}) collective-permute-start(bf16[1024,512]{1,0:T(8,128)(2,1)S(1)} %copy-done.3), channel_id=1, source_target_pairs={{0,8},{1,9},{2,10},{3,11},{4,12},{5,13},{6,14},{7,15},{8,0},{9,1},... | collective-permute-start | bytes 3145736 | tf_op jit(solution)/shard_map/ppermute | solution.py:264
  275.1 8.2 %collective-permute-start.27 = (bf16[1024,512]{1,0:T(8,128)(2,1)S(1)}, bf16[1024,512]{1,0:T(8,128)(2,1)S(1)}, u32[]{:S(2)}, u32[]{:S(2)}) collective-permute-start(bf16[1024,512]{1,0:T(8,128)(2,1)S(1)} %copy-done.5), channel_id=1, source_target_pairs={{0,8},{1,9},{2,10},{3,11},{4,12},{5,13},{6,14},{7,15},{8,0},{9,1},... | collective-permute-start | bytes 3145736 | tf_op jit(solution)/shard_map/ppermute | solution.py:264
  275.3 8.0 %collective-permute-start.29 = (bf16[1024,512]{1,0:T(8,128)(2,1)S(1)}, bf16[1024,512]{1,0:T(8,128)(2,1)S(1)}, u32[]{:S(2)}, u32[]{:S(2)}) collective-permute-start(bf16[1024,512]{1,0:T(8,128)(2,1)S(1)} %get-tuple-element.17.refs_6_), channel_id=1, source_target_pairs={{0,8},{1,9},{2,10},{3,11},{4,12},{5,13},{6,14},{7,15},{8,0},{9,1},... | collective-permute-start | bytes 3145736 | tf_op jit(solution)/shard_map/ppermute | solution.py:264
  275.6 7.7 %collective-permute-start.30 = (bf16[1024,512]{1,0:T(8,128)(2,1)S(1)}, bf16[1024,512]{1,0:T(8,128)(2,1)S(1)}, u32[]{:S(2)}, u32[]{:S(2)}) collective-permute-start(bf16[1024,512]{1,0:T(8,128)(2,1)S(1)} %get-tuple-element.18.refs_7_), channel_id=1, source_target_pairs={{0,8},{1,9},{2,10},{3,11},{4,12},{5,13},{6,14},{7,15},{8,0},{9,1},... | collective-permute-start | bytes 3145736 | tf_op jit(solution)/shard_map/ppermute | solution.py:264
  275.8 7.6 %collective-permute-start.31 = (f32[512,512]{1,0:T(8,128)S(1)}, f32[512,512]{1,0:T(8,128)S(1)}, u32[]{:S(2)}, u32[]{:S(2)}) collective-permute-start(f32[512,512]{1,0:T(8,128)S(1)} %get-tuple-element.19.refs_8_), channel_id=1, source_target_pairs={{0,8},{1,9},{2,10},{3,11},{4,12},{5,13},{6,14},{7,15},{8,0},{9,1},... | collective-permute-start | bytes 3145736 | tf_op jit(solution)/shard_map/ppermute | solution.py:264
  280.8 5.1 %copy-start.1 = (bf16[1024,512]{1,0:T(8,128)(2,1)S(1)}, bf16[1024,512]{1,0:T(8,128)(2,1)}, u32[]{:S(2)}) copy-start(bf16[1024,512]{1,0:T(8,128)(2,1)} %copy-done) | copy-start | bytes 3145732
  283.2 1.3 copy-start.12
  283.2 1.6 copy-start.13
  283.2 2.6 copy-start.14
  283.3 1.6 copy-start.15
  284.9 1.0 copy-start.16
